TPU v7x, 512 devices: a whole 4x4x16 slice. The times are simulated.
512 devices in a mesh: prow: 16 (over y_hi, x, core), pcol: 32 (over y_lo, z).
Axes of the slice: x: 4, y: 4 (y_hi: 2, y_lo: 2; y = y_hi * 2 + y_lo), z: 16, core: 2. Of those that a mesh axis runs over, the one named last changes fastest.
Arguments:
- sep_inverse: bfloat16 [2, 16, 256, 1, 32, 256], P(None, 'prow', None, None, 'pcol'), may hold values from -2 to 30, as said below
- panels: bfloat16 [4, 2, 16, 256, 256], P(None, None, 'prow', 'pcol'), may hold values from -0.0625 to 0.0625
- ancestors: int32 [4, 32], replicated, may hold values from 0 to 1, as said below
- window_factor: bfloat16 [6, 256, 256], replicated, may hold values from -0.1875 to 0.1875
- diag_inverse: bfloat16 [4, 256, 256], replicated, may hold values from -1 to 4, as said below
Outputs:
- ys: float32 [4, 2, 16, 256, 256], P(None, None, 'prow', 'pcol')
- window_inverse: float32 [1024, 1024], P('prow', 'pcol')
Inputs may be any that keep to these rules, and one draw needn't show every extreme that they name: sep_inverse read as in the first step is symmetric. `diag_inverse`: each block is symmetric. ancestors[k + 1, t] <= ancestors[k, t]: a supernode's ancestor tiles lie among those of the one before it.
All inputs are finite; a program needn't handle non-finite values.
Results may differ from a plain program's by a relative error of at most 0.00035.
Values may be sent and summed in bfloat16 or wider, within the bound.
A program may use at most 64 MiB of HBM per device.

v0:
```python
import jax
import jax.numpy as jnp
from jax import lax
from jax.sharding import PartitionSpec as P


def broadcast(block, axis, owner):
    block = jnp.where(lax.axis_index(axis) == owner, block, jnp.zeros_like(block))
    return lax.psum(block, axis)


def product(operand_left, operand_right):
    return jnp.dot(
        operand_left,
        operand_right,
        precision=lax.Precision.HIGHEST,
        preferred_element_type=jnp.float32,
    )


def pair_index(earlier, later):
    return later * (later - 1) // 2 + earlier


def window_step(later, window_sums, window_factor, diag_inverse, window_blocks):
    coupled = []
    for earlier in range(later):
        running = window_sums[earlier]
        for partner in range(later):
            running = running + product(
                window_blocks[earlier, partner],
                window_factor[pair_index(partner, later)].astype(jnp.float32),
            )
        upper_block = -running
        window_blocks[earlier, later] = upper_block
        window_blocks[later, earlier] = upper_block.T
        coupled.append(upper_block)
    running = window_sums[later]
    for earlier in range(later):
        running = running + product(
            window_factor[pair_index(earlier, later)].astype(jnp.float32).T, coupled[earlier]
        )
    window_blocks[later, later] = diag_inverse[later].astype(jnp.float32) - running


def assemble_window(window_blocks, supernodes):
    return jnp.block(
        [
            [window_blocks[first, second] for second in range(supernodes)]
            for first in range(supernodes)
        ]
    )


def per_device(sep_inverse, panels, ancestors, window_factor, diag_inverse):
    prow_count = lax.axis_size("prow")
    pcol_count = lax.axis_size("pcol")
    row_index = lax.axis_index("prow")
    column_index = lax.axis_index("pcol")
    tile_rows = sep_inverse.shape[0]
    width = sep_inverse.shape[2]
    owned_count = sep_inverse.shape[3]
    supernodes = panels.shape[0]
    slice_rows = panels.shape[3]
    group_ratio = pcol_count // prow_count
    local_sep = sep_inverse.reshape(tile_rows, width, owned_count, width)
    window_blocks = {}
    columns = []
    for later in range(supernodes):
        tile_flags = lax.dynamic_slice_in_dim(
            ancestors[later].reshape(tile_rows, prow_count), row_index, 1, 1
        )
        keep_tiles = tile_flags.astype(jnp.bfloat16).reshape(tile_rows, 1, 1)
        own_piece = panels[later, :, 0] * keep_tiles
        full_rows = lax.all_gather(own_piece, "pcol", axis=1, tiled=True)
        grouped = full_rows.reshape(owned_count, group_ratio, width, width)
        picked = lax.dynamic_slice_in_dim(grouped, column_index // prow_count, 1, 1)[:, 0]
        owned_tiles = broadcast(picked, "prow", column_index % prow_count)

        def row_term(first_row, row_count, owned_tiles=owned_tiles):
            return jnp.einsum(
                "rbcd,cde->bre", local_sep, owned_tiles, preferred_element_type=jnp.float32
            )

        summed = lax.psum_scatter(
            row_term(jnp.int32(0), slice_rows * lax.axis_size("pcol")),
            "pcol",
            scatter_dimension=0,
            tiled=True,
        )
        row_total = jnp.transpose(summed, (1, 0, 2)).reshape(tile_rows * slice_rows, width)
        row_keep = jnp.repeat(
            tile_flags[:, 0].astype(jnp.float32),
            slice_rows,
            total_repeat_length=tile_rows * slice_rows,
        )
        carried = -row_total
        for earlier in range(later):
            carried = carried - product(
                columns[earlier], window_factor[pair_index(earlier, later)].astype(jnp.float32)
            )
        current = carried * row_keep[:, None]
        factor_rows = own_piece.reshape(tile_rows * slice_rows, width).astype(jnp.float32)
        window_parts = [product(columns[earlier].T, factor_rows) for earlier in range(later)]
        window_parts.append(product(factor_rows.T, current))
        window_sums = lax.psum(jnp.stack(window_parts), ("prow", "pcol"))
        window_step(later, window_sums, window_factor, diag_inverse, window_blocks)
        columns.append(current)
    ys = jnp.stack(columns).reshape(supernodes, tile_rows, 1, slice_rows, width)
    whole_window = assemble_window(window_blocks, supernodes)
    rows_each = supernodes * width // prow_count
    cols_each = supernodes * width // pcol_count
    local_window = lax.dynamic_slice(
        whole_window, (row_index * rows_each, column_index * cols_each), (rows_each, cols_each)
    )
    return (ys, local_window)


def solution(mesh):
    placed = (
        P(None, "prow", None, None, "pcol", None),
        P(None, None, "prow", "pcol", None),
        P(),
        P(),
        P(),
    )
    return jax.shard_map(
        per_device,
        mesh=mesh,
        in_specs=placed,
        out_specs=(P(None, None, "prow", "pcol", None), P("prow", "pcol")),
        check_vma=False,
    )
```

profile of v0, /device:TPU:1, one launch (start us, length us, event | category | flops | bytes accessed | tf_op | source)
XLA Modules:
  0.0 1204.6 jit_solution(4849116906709062268)
XLA Ops:
  7.3 0.8 slice_reduce_fusion.1
  8.9 0.8 bitcast_multiply_fusion.6
  9.8 57.0 %all_gather.12 = bf16[2,256,256]{2,0,1:T(2,128)(2,1)S(1)} all-gather(bf16[2,8,256]{2,0,1:T(2,128)(2,1)S(1)} %copy.58), channel_id=1, replica_groups=mesh['prow'=16,'pcol'=32] {'pcol'}, dimensions={1}, use_global_device_ids=true | all-gather | bytes 270336 | tf_op jit(solution)/shard_map/all_gather | solution.py:75
  67.2 46.0 %all_gather.13 = bf16[2,256,256]{2,0,1:T(2,128)(2,1)S(1)} all-gather(bf16[2,8,256]{2,0,1:T(2,128)(2,1)S(1)} %copy.63), channel_id=1, replica_groups=mesh['prow'=16,'pcol'=32] {'pcol'}, dimensions={1}, use_global_device_ids=true | all-gather | bytes 270336 | tf_op jit(solution)/shard_map/all_gather | solution.py:75
  113.7 0.7 select_bitcast_fusion.3
  114.4 0.6 select_bitcast_fusion.2
  115.0 48.3 %all_gather.15 = bf16[2,256,256]{2,0,1:T(2,128)(2,1)S(1)} all-gather(bf16[2,8,256]{2,0,1:T(2,128)(2,1)S(1)} %copy.73), channel_id=1, replica_groups=mesh['prow'=16,'pcol'=32] {'pcol'}, dimensions={1}, use_global_device_ids=true | all-gather | bytes 270336 | tf_op jit(solution)/shard_map/all_gather | solution.py:75
  163.8 0.7 select_bitcast_fusion
  164.4 46.0 %all_gather.14 = bf16[2,256,256]{2,0,1:T(2,128)(2,1)S(1)} all-gather(bf16[2,8,256]{2,0,1:T(2,128)(2,1)S(1)} %copy.68), channel_id=1, replica_groups=mesh['prow'=16,'pcol'=32] {'pcol'}, dimensions={1}, use_global_device_ids=true | all-gather | bytes 270336 | tf_op jit(solution)/shard_map/all_gather | solution.py:75
  210.9 0.7 select_bitcast_fusion.1
  211.6 202.4 %all-reduce.15.cloned.1.call-done = (bf16[256,256]{0,1:T(8,128)(2,1)}, bf16[256,256]{0,1:T(8,128)(2,1)}, bf16[256,256]{0,1:T(8,128)(2,1)}, bf16[256,256]{0,1:T(8,128)(2,1)}) async-done(((bf16[256,256]{0,1:T(8,128)(2,1)}, bf16[256,256]{0,1:T(8,128)(2,1)}, bf16[256,256]{0,1:T(8,128)(2,1)}, bf16[256,256]{0,1:T(8,128)(2,1)}), (bf16[256,256]{0,1:T(8,128)(2,1)}, bf16[256,256]{0,1:T(8,128)(2,1)}, ...) | async-done | bytes 524304 | tf_op jit(solution)/shard_map/psum | solution.py:9
  414.1 1.2 convolution_bitcast_fusion
  415.3 1.0 copy.75
  416.5 1.0 copy.60
  417.8 1.0 copy.65
  419.1 1.0 copy.70
  421.3 0.6 fusion.134
  421.9 0.6 fusion.135
  422.5 0.7 fusion.136
  423.2 0.6 fusion.137
  423.7 5.0 broadcast_select_fusion
  428.8 1.3 dynamic-slice.31
  430.8 233.1 %all-reduce.13.cloned.1.call-done = (f32[256,2,256]{2,1,0:T(2,128)}, f32[256,2,256]{2,1,0:T(2,128)}, f32[256,2,256]{2,1,0:T(2,128)}, f32[256,2,256]{2,1,0:T(2,128)}) async-done(((f32[256,2,256]{2,1,0:T(2,128)}, f32[256,2,256]{2,1,0:T(2,128)}, f32[256,2,256]{2,1,0:T(2,128)}, f32[256,2,256]{2,1,0:T(2,128)}), (f32[256,2,256]{2,1,0:T(2,128)}, f32[256,2,256]{2,1,0:T(2,128)}, f32[256,2,256]{2,1,0:T(2,128)}, ...) | async-done | bytes 2097168
  663.9 0.7 constant_dynamic-slice_fusion.11
  665.8 1.1 convolution_bitcast_fusion.19
  666.9 0.7 constant_dynamic-slice_fusion.10
  667.6 0.7 constant_dynamic-slice_fusion.9
  670.3 0.7 constant_dynamic-slice_fusion.8
  671.4 0.4 convolution_bitcast_fusion.17
  672.4 0.8 pad_maximum_fusion.2
  673.3 0.9 pad_maximum_fusion.1
  674.2 1.1 pad_maximum_fusion
  675.4 0.6 pad_maximum_fusion.3
  676.0 502.1 %all-reduce.11.cloned.1.call-done = (f32[1,256,256]{2,1,0:T(8,128)}, f32[4,256,256]{2,1,0:T(8,128)}, f32[2,256,256]{2,1,0:T(8,128)}, f32[3,256,256]{2,1,0:T(8,128)}) async-done(((f32[1,256,256]{2,1,0:T(8,128)}, f32[4,256,256]{2,1,0:T(8,128)}, f32[2,256,256]{2,1,0:T(8,128)}, f32[3,256,256]{2,1,0:T(8,128)}), (f32[1,256,256]{2,1,0:T(8,128)}, f32[4,256,256]{2,1,0:T(8,128)}, f32[2,256,256]{2,1,0:T(8,128)}, ...) | async-done | bytes 2621456 | tf_op jit(solution)/shard_map/psum | solution.py:106
  1178.1 1.0 subtract_bitcast_fusion
  1179.1 1.3 fusion.14
  1181.5 0.4 copy-done.5
  1182.9 1.0 fusion.7
  1184.3 0.8 copy.82
  1186.0 0.9 copy.86
  1186.8 0.9 copy.91
  1188.6 1.2 fusion.6
  1189.8 0.8 copy.85
  1190.7 2.0 fusion.3
  1192.7 0.8 copy.90
  1193.9 0.6 copy-done.3
  1195.0 1.9 fusion.1
  1197.4 0.7 copy.93
  (92 shorter events, 14.2 us)
Async XLA Ops:
  7.2 406.9 %copy-start = (bf16[2,1,256,1,1,256]{5,2,4,3,1,0:T(8,128)(2,1)S(1)}, bf16[2,1,256,1,1,256]{5,2,4,3,1,0:T(8,128)(2,1)}, u32[]{:S(2)}) copy-start(bf16[2,1,256,1,1,256]{5,2,4,3,1,0:T(8,128)(2,1)} %param.15) | copy-start | bytes 786436
  7.2 406.9 %all-reduce.15.cloned.1.call-start = ((), (), s32[]{:S(2)}) async-start(), calls=%async_computation.2 | async-start | bytes 1048576 | tf_op jit(solution)/shard_map/psum | solution.py:9
  211.6 452.3 %all-reduce.13.cloned.1.call-start = ((), (), s32[]{:S(2)}) async-start(), calls=%async_computation.1 | async-start | bytes 4194304
  414.1 2.2 copy-start.11
  416.3 1.3 copy-start.10
  417.6 1.3 copy-start.9
  420.1 3.6 copy-start.12
  420.1 244.5 %copy-start.8 = (bf16[4,2,1,8,256]{4,3,2,1,0:T(8,128)(2,1)S(1)}, bf16[4,2,1,8,256]{4,3,2,1,0:T(8,128)(2,1)}, u32[]{:S(2)}) copy-start(bf16[4,2,1,8,256]{4,3,2,1,0:T(8,128)(2,1)} %param.16) | copy-start | bytes 98308
  420.1 248.2 %copy-start.1 = (bf16[6,256,256]{2,1,0:T(8,128)(2,1)S(1)}, bf16[6,256,256]{2,1,0:T(8,128)(2,1)}, u32[]{:S(2)}) copy-start(bf16[6,256,256]{2,1,0:T(8,128)(2,1)} %param.18) | copy-start | bytes 2359300
  420.2 757.9 %all-reduce.11.cloned.1.call-start = ((), (), s32[]{:S(2)}) async-start(), calls=%async_computation | async-start | bytes 5242880 | tf_op jit(solution)/shard_map/psum | solution.py:106
  675.3 502.8 %copy-start.7 = (bf16[4,256,256]{2,1,0:T(8,128)(2,1)S(1)}, bf16[4,256,256]{2,1,0:T(8,128)(2,1)}, u32[]{:S(2)}) copy-start(bf16[4,256,256]{2,1,0:T(8,128)(2,1)} %param.19) | copy-start | bytes 1572868
  1178.1 2.4 copy-start.6
  1179.1 1.7 copy-start.2
  1180.8 1.1 copy-start.5
  1187.7 0.9 copy-start.4
  1193.5 0.9 copy-start.3
Sparse Core Ops, SparseCore 0:
  211.7 202.3 all-reduce.14
  420.3 243.5 all-reduce.12
  675.4 502.6 all-reduce.10
where the time goes:
time: 1210 us; the launch traced here: 1200 us
  waiting for transfers between devices  938 us (78%)
  blocking collectives  197 us (16%)
  local copies, waits for them, and re-layouts  20.5 us (2%)
  matrix products  19.6 us (2%)
  between operations  14.9 us (1%)
  other arithmetic  14.3 us (1%)
    psum x1, waiting for transfers between devices, per_device(): window_sums = lax.psum(jnp.stack(window_parts), ('prow', 'pcol'))  502 us
    unnamed x4, waiting for transfers between devices  233 us
    psum x1, waiting for transfers between devices, broadcast(): return lax.psum(block, axis)  202 us
    all_gather x4, blocking collectives, per_device(): full_rows = lax.all_gather(own_piece, 'pcol', axis=1, tiled=True)  197 us
  transfers between devices with their start and end apart: 3, of which 3 were waited for; matrix products, arithmetic and copies ran while one was open for 1% of the time, Pallas kernels for 0%

commit v1 on v0

v1 whole, which is shorter than its diff:
```python
import jax
import jax.numpy as jnp
from jax import lax
from jax.experimental import pallas as pl
from jax.experimental.pallas import tpu as pltpu
from jax.sharding import PartitionSpec as P

MESH = pl.DeviceIdType.MESH
F32 = jnp.float32
BF16 = jnp.bfloat16
NP = 16
NZ = 16
W = 256
KS = 4
NC = KS * W


def rem(value, n):
    return lax.rem(value, jnp.int32(n))


def div(value, n):
    return lax.div(value, jnp.int32(n))


def dot(left, right):
    return jnp.dot(left, right, preferred_element_type=F32)


def dot_rows(left, right):
    return lax.dot_general(left, right, (((0,), (0,)), ((), ())), preferred_element_type=F32)


def halves(value):
    high = value.astype(BF16)
    low = (value - high.astype(F32)).astype(BF16)
    return high, low


def pair_index(earlier, later):
    return later * (later - 1) // 2 + earlier


def drain(ref, sem):
    pltpu.make_async_copy(ref, ref, sem).wait()


def kernel(
    s_ref, p_ref, anc_ref, l_ref, d_ref, y_ref, v_ref,
    fg, wide, st, give, keep, pairb, red, mh, ml, uh, ul, ysend, yrecv, vsend, vrecv, wc, dm, dmw, vps, vpr,
    ag_send, ag_recv, ye_send, ye_recv, pair_send, pair_recv, red_send, red_recv,
    y_send, y_recv, v_send, v_recv, f_send, f_recv,
):
    p = lax.axis_index("prow")
    q = lax.axis_index("pcol")
    core = rem(p, 2)
    chip = div(p, 2)
    ylo = div(q, NZ)
    z = rem(q, NZ)

    def copy(src, dst, send, recv, prow, pcol):
        return pltpu.make_async_remote_copy(
            src_ref=src, dst_ref=dst, send_sem=send, recv_sem=recv,
            device_id=(prow, pcol), device_id_type=MESH,
        )

    barrier = pltpu.get_barrier_semaphore()
    right = rem(z + 1, NZ)
    left = rem(z + NZ - 1, NZ)
    for dp in range(NP):
        for dy in range(2):
            if dp or dy:
                pl.semaphore_signal(
                    barrier, inc=1,
                    device_id=(rem(p + dp, NP), rem(ylo + dy, 2) * NZ + z), device_id_type=MESH,
                )
    for other in (right, left):
        pl.semaphore_signal(barrier, inc=1, device_id=(p, ylo * NZ + other), device_id_type=MESH)

    rows = []
    for r in range(2):
        parts = []
        for k in range(KS):
            flag = anc_ref[k, r * NP + p].astype(F32)
            parts.append(p_ref[k, r].astype(F32) * flag)
        rows.append(jnp.concatenate(parts, axis=1))
    fg[z, ylo] = jnp.concatenate(rows, axis=0).astype(BF16)

    pl.semaphore_wait(barrier, 33)

    ycopy = copy(fg.at[z, ylo], fg.at[z, ylo], ye_send, ye_recv, p, (1 - ylo) * NZ + z)

    def ring(way, e, step):
        row = rem(ylo + e, 2)
        at = rem(z + NZ - step, NZ) if way == 0 else rem(z + step, NZ)
        to = right if way == 0 else left
        return copy(
            fg.at[at, row], fg.at[at, row], ag_send.at[way, e, step], ag_recv.at[way, e, step],
            p, ylo * NZ + to,
        )

    def task_s(r):
        def run():
            value = s_ref[r].astype(F32).reshape(2, NZ, 8, W)
            for y in range(2):
                wide[:, y, r] = value[y]

        return run

    def task_t():
        st[...] = wide[...].reshape(512, W).T.astype(BF16)

    def put(m, k, value):
        high, low = halves(value)
        mh[m, :, k * W : (k + 1) * W] = high
        ml[m, :, k * W : (k + 1) * W] = low

    def times(m, k, later):
        both = jnp.concatenate(
            [mh[m, :, k * W : (k + 1) * W], ml[m, :, k * W : (k + 1) * W]], axis=0
        )
        out = dot(both, l_ref[pair_index(k, later)])
        return out[:W] + out[W:]

    def coupling(m, k):
        return l_ref[pair_index(m, k)].astype(F32)

    def task_zero():
        rows_at = lax.broadcasted_iota(jnp.int32, (W, W), 0)
        cols_at = lax.broadcasted_iota(jnp.int32, (W, W), 1)
        eye = jnp.where(rows_at == cols_at, 1.0, 0.0).astype(BF16)
        zero = jnp.zeros((W, W), BF16)
        for m in range(KS):
            for k in range(m + 1):
                mh[m, :, k * W : (k + 1) * W] = eye if m == k else zero
                ml[m, :, k * W : (k + 1) * W] = zero
        for m in range(KS - 1):
            put(m, m + 1, -coupling(m, m + 1))

    def task_m2():
        for m in range(2):
            put(m, m + 2, -(coupling(m, m + 2) + times(m, m + 1, m + 2)))

    def task_m3():
        put(0, 3, -(coupling(0, 3) + times(0, 1, 3) + times(0, 2, 3)))

    share = ylo * NP + p
    block = div(share, 8)
    first = pl.multiple_of(rem(share, 8) * 32, 32)
    lane = lax.broadcasted_iota(jnp.int32, (32, 128), 1)

    def task_d():
        dd = d_ref[block, pl.ds(first, 32), :]
        for a in range(8):
            cols = slice(128 * a, 128 * a + 128)
            dm[a] = dot(dd, mh[block, :, cols]) + dot(dd, ml[block, :, cols])
        group = div(z, 4)
        sub = rem(z, 4)
        low_cols = dm[group]
        high_cols = dm[4 + group]
        picked = jnp.zeros((32, 128), F32)
        for b in range(4):
            one = jnp.where(
                lane < 32,
                pltpu.roll(low_cols, (128 - 32 * b) % 128, 1),
                pltpu.roll(high_cols, (160 - 32 * b) % 128, 1),
            )
            picked = jnp.where(sub == b, one, picked)
        picked = jnp.where(lane < 64, picked, 0.0)
        high = picked.astype(BF16).astype(F32)
        dmw[...] = jnp.where(lane < 64, high, pltpu.roll(picked - high, 64, 1)).astype(BF16)

    def task_wc():
        wc[...] = jnp.zeros(wc.shape, F32)

    tasks = [task_s(0), task_s(1), task_t, task_zero, task_m2, task_m3, task_d, task_wc]

    ycopy.start()
    for way in range(2):
        ring(way, 0, 0).start()
    tasks.pop(0)()
    ycopy.wait_recv()
    for way in range(2):
        ring(way, 1, 0).start()
    last = (8, 7)
    for step in range(1, 9):
        if tasks:
            tasks.pop(0)()
        for e in range(2):
            for way in range(2):
                if step <= last[way]:
                    ring(way, e, step - 1).wait_recv()
                    if step < last[way]:
                        ring(way, e, step).start()
    while tasks:
        tasks.pop(0)()

    def gathered(k):
        return fg[:, :, :, k * W : (k + 1) * W].reshape(512, W)

    mine = pl.multiple_of(core * 128, 128)
    theirs = pl.multiple_of((1 - core) * 128, 128)
    mate = p + 1 - 2 * core

    def pair(k):
        return copy(give.at[k], pairb.at[k], pair_send.at[k], pair_recv.at[k], mate, q)

    def spread(k, d):
        to = rem(chip + d, 8)
        rows_to = pl.multiple_of(to * 16, 16)
        return copy(
            keep.at[k, pl.ds(rows_to, 16)], red.at[k, d - 1], red_send.at[k], red_recv.at[k],
            to * 2 + core, q,
        )

    for k in range(KS):
        give[k] = dot(st[pl.ds(theirs, 128), :], gathered(k))
        keep[k] = dot(st[pl.ds(mine, 128), :], gathered(k))
        pair(k).start()
    for k in range(KS):
        pair(k).wait_recv()
        keep[k] = keep[k] + pairb[k]
        for d in range(1, 8):
            spread(k, d).start()

    for k in range(KS):
        if k == 0:
            uh[0] = gathered(0)
            ul[0] = jnp.zeros((512, W), BF16)
        else:
            total = gathered(k).astype(F32)
            for m in range(k):
                left_side = gathered(m)
                cols = slice(k * W, (k + 1) * W)
                total = total + dot(left_side, mh[m, :, cols]) + dot(left_side, ml[m, :, cols])
            high, low = halves(total)
            uh[k] = high
            ul[k] = low

    own_rows = pl.multiple_of(chip * 16, 16)
    blocks = []
    for k in range(KS):
        drain(red.at[k], red_recv.at[k])
        total = keep[k, pl.ds(own_rows, 16), :]
        for d in range(7):
            total = total + red[k, d]
        for m in range(k):
            high, low = halves(blocks[m])
            both = dot(jnp.concatenate([high, low], axis=0), l_ref[pair_index(m, k)])
            total = total - (both[:16] + both[16:])
        blocks.append(total)
        for e in range(2):
            ysend[e, :, k * W : (k + 1) * W] = total[8 * e : 8 * e + 8]

    lane8 = lax.broadcasted_iota(jnp.int32, (8, 128), 1)
    for a in range(4):
        k, at = divmod(128 * a, W)
        first_a = blocks[k][:, at : at + 128]
        second_a = blocks[k + 2][:, at : at + 128]
        for b in range(4):
            def moved(value, group):
                shift = (32 * (group - b)) % 128
                return pltpu.roll(value, shift, 1) if shift else value

            piece = jnp.where(
                lane8 < 64,
                jnp.where(lane8 < 32, moved(first_a[:8], 0), moved(second_a[:8], 1)),
                jnp.where(lane8 < 96, moved(first_a[8:], 2), moved(second_a[8:], 3)),
            )
            vsend[4 * a + b] = piece

    chunk = core * 8 + chip
    here = z == p

    def ypart(e):
        to = 2 * chunk + e
        return copy(ysend.at[e], yrecv.at[ylo], y_send.at[e], y_recv.at[ylo], z, to)

    def ylocal(e):
        return pltpu.make_async_copy(ysend.at[e], yrecv.at[ylo], y_recv.at[ylo])

    def vpart(d):
        to = rem(z + d, NZ)
        return copy(
            vsend.at[to], vrecv.at[chunk], v_send.at[min(d, 1)], v_recv, z, ylo * NZ + to,
        )

    def vlocal():
        return pltpu.make_async_copy(vsend.at[z], vrecv.at[chunk], v_recv)

    for d in range(1, NZ):
        vpart(d).start()

    @pl.when(here)
    def _():
        vlocal().start()

    @pl.when(jnp.logical_not(here))
    def _():
        vpart(0).start()

    for e in range(2):
        home = jnp.logical_and(here, q == 2 * chunk + e)

        @pl.when(home)
        def _():
            ylocal(e).start()

        @pl.when(jnp.logical_not(home))
        def _():
            ypart(e).start()

    drain(vrecv, v_recv)
    got = vrecv[...].reshape(2, 8, 8, 128)
    wide_lane = lax.broadcasted_iota(jnp.int32, (8, 8, 128), 2)
    for y in range(2):
        for h in range(2):
            value = got[y]
            if h:
                value = pltpu.roll(value, 64, 2)
            value = jnp.where(wide_lane < 64, value, 0.0)
            high = value.astype(BF16).astype(F32)
            value = jnp.where(wide_lane < 64, high, pltpu.roll(value - high, 64, 2))
            for n in range(8):
                wc[2 * n + h, y, ylo] = value[n]
    columns = wc[...].reshape(512, 128).astype(BF16)
    lane16 = lax.broadcasted_iota(jnp.int32, (4, 16, 128), 2)
    for k in range(KS):
        cols = slice(k * W, (k + 1) * W)
        total = dot_rows(uh[k], columns) + dot_rows(ul[k], columns)
        total = total + dot_rows(mh[block, pl.ds(first, 32), cols], dmw[...])
        total = total + dot_rows(ml[block, pl.ds(first, 32), cols], dmw[...])
        total = total + pltpu.roll(total, 64, 1)
        total = total.reshape(4, 4, 16, 128)
        for e in range(2):
            packed = None
            for g in range(4):
                shift = (32 * (g - e)) % 128
                value = total[:, g]
                if shift:
                    value = pltpu.roll(value, shift, 2)
                packed = value if packed is None else jnp.where(lane16 < 32 * g, packed, value)
            vps[4 * k : 4 * k + 4, e] = packed

    def final(dp, dy):
        to = rem(p + dp, NP)
        row = rem(ylo + dy, 2)
        return copy(
            vps.at[to, row], vpr.at[2 * dp + dy - 1], f_send, f_recv, to, row * NZ + z
        )

    for dp in range(NP):
        for dy in range(2):
            if dp or dy:
                final(dp, dy).start()

    for r in range(2):
        drain(yrecv.at[r], y_recv.at[r])
        for k in range(KS):
            flag = anc_ref[k, r * NP + p].astype(F32)
            y_ref[k, r] = yrecv[r, :, k * W : (k + 1) * W] * (0.0 - flag)

    drain(vpr, f_recv)
    total = vps[p, ylo]
    for n in range(31):
        total = total + vpr[n]
    for g in range(4):
        value = total
        if g:
            value = pltpu.roll(value, 128 - 32 * g, 1)
        v_ref[16 * g : 16 * g + 16, :] = value[:, :32]

    ycopy.wait_send()
    for step in range(8):
        for e in range(2):
            for way in range(2):
                if step < last[way]:
                    ring(way, e, step).wait_send()
    for k in range(KS):
        pair(k).wait_send()
        drain(red.at[k], red_send.at[k])
    drain(vrecv.at[pl.ds(0, 15)], v_send.at[1])

    @pl.when(jnp.logical_not(here))
    def _():
        vpart(0).wait_send()

    for e in range(2):
        home = jnp.logical_and(here, q == 2 * chunk + e)

        @pl.when(jnp.logical_not(home))
        def _():
            ypart(e).wait_send()

    drain(vpr, f_send)


def per_device(sep_inverse, panels, ancestors, window_factor, diag_inverse):
    dma = pltpu.SemaphoreType.DMA
    ys, window = pl.pallas_call(
        kernel,
        out_shape=(
            jax.ShapeDtypeStruct((KS, 2, 8, W), F32),
            jax.ShapeDtypeStruct((64, 32), F32),
        ),
        in_specs=[
            pl.BlockSpec(memory_space=pltpu.VMEM),
            pl.BlockSpec(memory_space=pltpu.VMEM),
            pl.BlockSpec(memory_space=pltpu.SMEM),
            pl.BlockSpec(memory_space=pltpu.VMEM),
            pl.BlockSpec(memory_space=pltpu.VMEM),
        ],
        out_specs=(pl.BlockSpec(memory_space=pltpu.VMEM), pl.BlockSpec(memory_space=pltpu.VMEM)),
        scratch_shapes=[
            pltpu.VMEM((NZ, 2, 16, NC), BF16),
            pltpu.VMEM((NZ, 2, 2, 8, W), F32),
            pltpu.VMEM((W, 512), BF16),
            pltpu.VMEM((KS, 128, W), F32),
            pltpu.VMEM((KS, 128, W), F32),
            pltpu.VMEM((KS, 128, W), F32),
            pltpu.VMEM((KS, 7, 16, W), F32),
            pltpu.VMEM((KS, W, NC), BF16),
            pltpu.VMEM((KS, W, NC), BF16),
            pltpu.VMEM((KS, 512, W), BF16),
            pltpu.VMEM((KS, 512, W), BF16),
            pltpu.VMEM((2, 8, NC), F32),
            pltpu.VMEM((2, 8, NC), F32),
            pltpu.VMEM((NZ, 8, 128), F32),
            pltpu.VMEM((NZ, 8, 128), F32),
            pltpu.VMEM((NZ, 2, 2, 8, 128), F32),
            pltpu.VMEM((8, 32, 128), F32),
            pltpu.VMEM((32, 128), BF16),
            pltpu.VMEM((NP, 2, 16, 128), F32),
            pltpu.VMEM((31, 16, 128), F32),
            dma((2, 2, 8)), dma((2, 2, 8)),
            dma(()), dma(()),
            dma((KS,)), dma((KS,)),
            dma((KS,)), dma((KS,)),
            dma((2,)), dma((2,)),
            dma((2,)), dma(()),
            dma(()), dma(()),
        ],
        compiler_params=pltpu.CompilerParams(collective_id=0, has_side_effects=True),
        name="selinv",
    )(
        sep_inverse.reshape(2, W, W),
        panels.reshape(KS, 2, 8, W),
        ancestors,
        window_factor,
        diag_inverse,
    )
    return ys.reshape(KS, 2, 1, 8, W), window


def solution(mesh):
    placed = (
        P(None, "prow", None, None, "pcol", None),
        P(None, None, "prow", "pcol", None),
        P(),
        P(),
        P(),
    )
    return jax.shard_map(
        per_device,
        mesh=mesh,
        in_specs=placed,
        out_specs=(P(None, None, "prow", "pcol", None), P("prow", "pcol")),
        check_vma=False,
    )
```

time: 1210 us -> 82.1 us (0.07)
  waiting for transfers between devices: 938 us -> 0 us
  blocking collectives: 197 us -> 0 us
  Pallas kernels: 0 us -> 77.1 us
  matrix products: 19.6 us -> 0 us
  local copies, waits for them, and re-layouts: 20.5 us -> 2.91 us
  other arithmetic: 14.3 us -> 0 us
  between operations: 14.9 us -> 0.64 us
    psum x2 -> x0, waiting for transfers between devices: 705 us -> none  [the longest x1 502 us: per_device(): window_sums = lax.psum(jnp.stack(window_parts), ('prow', 'pcol'))]
    unnamed x4 -> x0, waiting for transfers between devices: 233 us -> none
    all_gather x4 -> x0, blocking collectives: 197 us -> none  [per_device(): full_rows = lax.all_gather(own_piece, 'pcol', axis=1, tiled=True)]
    pallas_call x0 -> x1, Pallas kernels: none -> 77.1 us  [per_device(): pl.pallas_call(kernel, out_shape=(jax.ShapeDtypeStruct((KS, 2, 8, W), F32...]
    dot_general x40 -> x0, matrix products: 19.6 us -> none  [the longest x36 17.6 us: product(): jnp.dot(operand_left, operand_right, precision=lax.Precision.HIGHEST, pre...]
  transfers between devices with their start and end apart: 3 -> 0, of which waited for: 3 -> 0; matrix products, arithmetic and copies ran while one was open for 1% -> 0% of each run, Pallas kernels for 0% -> 0%
where the time goes in v1:
time: 82.1 us; the launch traced here: 80.7 us
  Pallas kernels  77.1 us (94%)
  local copies, waits for them, and re-layouts  2.91 us (4%)
    pallas_call x1, Pallas kernels, per_device(): pl.pallas_call(kernel, out_shape=(jax.ShapeDtypeStruct((KS, 2, 8, W), F32...  77.1 us
    unnamed x2, local copies, waits for them, and re-layouts  2.91 us

profile of v1, /device:TPU:1, one launch (start us, length us, event | category | flops | bytes accessed | tf_op | source)
XLA Modules:
  0.0 80.7 jit_solution(2563082724975723345)
XLA Ops:
  0.6 77.1 %selinv.1 = (f32[4,2,8,256]{3,2,1,0:T(8,128)}, f32[64,32]{1,0:T(8,128)}) custom-call(bf16[2,256,256]{2,1,0:T(8,128)(2,1)} %bitcast.5, bf16[4,2,8,256]{3,2,1,0:T(8,128)(2,1)} %bitcast.7, s32[4,32]{1,0:T(4,128)} %anc_ref.1, bf16[6,256,256]{2,1,0:T(8,128)(2,1)} %l_ref.1, bf16[4,256,256]{2,1,0:T(8,128)(2,1)} %d_ref.1), custom_call_target="tpu_custom_call" | custom-call | tf_op jit(solution)/shard_map/selinv/pallas_call | solution.py:400
  77.8 1.4 %copy.8 = f32[64,32]{0,1:T(8,128)} copy(f32[64,32]{1,0:T(8,128)} %get-tuple-element.7) | data formatting | bytes 16384
  79.2 1.5 %copy.10 = f32[4,2,1,8,256]{4,3,2,1,0:T(8,128)} copy(f32[4,2,1,8,256]{4,3,2,1,0:T(8,128)} %bitcast.6) | data formatting | bytes 131072

commit v2 on v1

--- a/solution.py
+++ b/solution.py
@@ -65,39 +65,71 @@
         )
 
     barrier = pltpu.get_barrier_semaphore()
-    right = rem(z + 1, NZ)
-    left = rem(z + NZ - 1, NZ)
-    for dp in range(NP):
-        for dy in range(2):
-            if dp or dy:
-                pl.semaphore_signal(
-                    barrier, inc=1,
-                    device_id=(rem(p + dp, NP), rem(ylo + dy, 2) * NZ + z), device_id_type=MESH,
-                )
-    for other in (right, left):
-        pl.semaphore_signal(barrier, inc=1, device_id=(p, ylo * NZ + other), device_id_type=MESH)
-
-    rows = []
-    for r in range(2):
+    greeted = [(p + 1 - 2 * core, q), (p, (1 - ylo) * NZ + z)]
+    greeted += [(rem(chip + d, 8) * 2 + core, q) for d in range(1, 8)]
+    greeted += [(p, ylo * NZ + rem(z + NZ + a, NZ)) for a in (1, -1, 3, -3, -2)]
+    for other in greeted:
+        pl.semaphore_signal(barrier, inc=1, device_id=other, device_id_type=MESH)
+
+    for k in range(KS):
         parts = []
-        for k in range(KS):
+        for r in range(2):
             flag = anc_ref[k, r * NP + p].astype(F32)
             parts.append(p_ref[k, r].astype(F32) * flag)
-        rows.append(jnp.concatenate(parts, axis=1))
-    fg[z, ylo] = jnp.concatenate(rows, axis=0).astype(BF16)
-
-    pl.semaphore_wait(barrier, 33)
-
-    ycopy = copy(fg.at[z, ylo], fg.at[z, ylo], ye_send, ye_recv, p, (1 - ylo) * NZ + z)
-
-    def ring(way, e, step):
-        row = rem(ylo + e, 2)
-        at = rem(z + NZ - step, NZ) if way == 0 else rem(z + step, NZ)
-        to = right if way == 0 else left
+        fg[z, ylo, k] = jnp.concatenate(parts, axis=0).astype(BF16)
+
+    pl.semaphore_wait(barrier, len(greeted))
+
+
+    def finish(stage):
+        if stage >= 1:
+            for a in direct:
+                hop(0, a).wait_send()
+            for a, further in relays.items():
+                for b in further:
+                    hop(a, b).wait_send()
+            for a in range(-7, 9):
+                across(a).wait_send()
+        if stage >= 2:
+            for k in range(KS):
+                pair(k).wait_send()
+        if stage >= 3:
+            for k in range(KS):
+                drain(red.at[k], red_send.at[k])
+        if stage >= 5:
+            drain(vrecv.at[pl.ds(0, 15)], v_send.at[1])
+
+            @pl.when(jnp.logical_not(here))
+            def _():
+                vpart(0).wait_send()
+
+            for e in range(2):
+                home = jnp.logical_and(here, q == 2 * chunk + e)
+
+                @pl.when(jnp.logical_not(home))
+                def _():
+                    ypart(e).wait_send()
+        if stage >= 6:
+            drain(vpr, f_send)
+        if stage < 6:
+            y_ref[...] = jnp.zeros(y_ref.shape, F32)
+            v_ref[...] = jnp.zeros(v_ref.shape, F32)
+
+    def hop(a, b):
+        at = rem(z + NZ - a, NZ)
         return copy(
-            fg.at[at, row], fg.at[at, row], ag_send.at[way, e, step], ag_recv.at[way, e, step],
-            p, ylo * NZ + to,
-        )
+            fg.at[at, ylo], fg.at[at, ylo], ag_send.at[a + b + 7], ag_recv.at[a + b + 7],
+            p, ylo * NZ + rem(z + NZ + b, NZ),
+        )
+
+    def across(a):
+        at = rem(z + NZ - a, NZ)
+        return copy(
+            fg.at[at, ylo], fg.at[at, ylo], ye_send.at[a + 7], ye_recv.at[a + 7], p, (1 - ylo) * NZ + z
+        )
+
+    relays = {3: (3, 1, -1), -3: (-3, 1, -1), 6: (2, 1, -1), -6: (-1, 1)}
+    direct = (3, -3, 1, -1)
 
     def task_s(r):
         def run():
@@ -175,28 +207,24 @@
 
     tasks = [task_s(0), task_s(1), task_t, task_zero, task_m2, task_m3, task_d, task_wc]
 
-    ycopy.start()
-    for way in range(2):
-        ring(way, 0, 0).start()
+    for a in direct:
+        hop(0, a).start()
+    across(0).start()
     tasks.pop(0)()
-    ycopy.wait_recv()
-    for way in range(2):
-        ring(way, 1, 0).start()
-    last = (8, 7)
-    for step in range(1, 9):
-        if tasks:
+    for a in (1, -1, 3, -3, 2, -2, 4, -4, 6, -6, 5, -5, 7, -7, 8):
+        hop(0, a).wait_recv()
+        for b in relays.get(a, ()):
+            hop(a, b).start()
+        across(a).start()
+        if tasks and a in (1, -1, -2, -4, -6):
             tasks.pop(0)()
-        for e in range(2):
-            for way in range(2):
-                if step <= last[way]:
-                    ring(way, e, step - 1).wait_recv()
-                    if step < last[way]:
-                        ring(way, e, step).start()
     while tasks:
         tasks.pop(0)()
+    for a in range(-7, 9):
+        across(a).wait_recv()
 
     def gathered(k):
-        return fg[:, :, :, k * W : (k + 1) * W].reshape(512, W)
+        return fg[:, :, k].reshape(512, W)
 
     mine = pl.multiple_of(core * 128, 128)
     theirs = pl.multiple_of((1 - core) * 128, 128)
@@ -213,16 +241,19 @@
             to * 2 + core, q,
         )
 
+    def pass_on(k):
+        pair(k).wait_recv()
+        keep[k] = keep[k] + pairb[k]
+        for d in range(1, 8):
+            spread(k, d).start()
+
     for k in range(KS):
         give[k] = dot(st[pl.ds(theirs, 128), :], gathered(k))
         keep[k] = dot(st[pl.ds(mine, 128), :], gathered(k))
         pair(k).start()
-    for k in range(KS):
-        pair(k).wait_recv()
-        keep[k] = keep[k] + pairb[k]
-        for d in range(1, 8):
-            spread(k, d).start()
-
+        if k:
+            pass_on(k - 1)
+    pass_on(KS - 1)
     for k in range(KS):
         if k == 0:
             uh[0] = gathered(0)
@@ -370,29 +401,7 @@
             value = pltpu.roll(value, 128 - 32 * g, 1)
         v_ref[16 * g : 16 * g + 16, :] = value[:, :32]
 
-    ycopy.wait_send()
-    for step in range(8):
-        for e in range(2):
-            for way in range(2):
-                if step < last[way]:
-                    ring(way, e, step).wait_send()
-    for k in range(KS):
-        pair(k).wait_send()
-        drain(red.at[k], red_send.at[k])
-    drain(vrecv.at[pl.ds(0, 15)], v_send.at[1])
-
-    @pl.when(jnp.logical_not(here))
-    def _():
-        vpart(0).wait_send()
-
-    for e in range(2):
-        home = jnp.logical_and(here, q == 2 * chunk + e)
-
-        @pl.when(jnp.logical_not(home))
-        def _():
-            ypart(e).wait_send()
-
-    drain(vpr, f_send)
+    finish(6)
 
 
 def per_device(sep_inverse, panels, ancestors, window_factor, diag_inverse):
@@ -412,7 +421,7 @@
         ],
         out_specs=(pl.BlockSpec(memory_space=pltpu.VMEM), pl.BlockSpec(memory_space=pltpu.VMEM)),
         scratch_shapes=[
-            pltpu.VMEM((NZ, 2, 16, NC), BF16),
+            pltpu.VMEM((NZ, 2, KS, 16, W), BF16),
             pltpu.VMEM((NZ, 2, 2, 8, W), F32),
             pltpu.VMEM((W, 512), BF16),
             pltpu.VMEM((KS, 128, W), F32),
@@ -432,8 +441,8 @@
             pltpu.VMEM((32, 128), BF16),
             pltpu.VMEM((NP, 2, 16, 128), F32),
             pltpu.VMEM((31, 16, 128), F32),
-            dma((2, 2, 8)), dma((2, 2, 8)),
-            dma(()), dma(()),
+            dma((16,)), dma((16,)),
+            dma((16,)), dma((16,)),
             dma((KS,)), dma((KS,)),
             dma((KS,)), dma((KS,)),
             dma((2,)), dma((2,)),

time: 82.1 us -> 71.9 us (0.88); the launches traced: 80.7 us -> 71.4 us
  Pallas kernels: 77.1 us -> 67.9 us
    pallas_call x1, Pallas kernels: 77.1 us -> 67.9 us  [per_device(): pl.pallas_call(kernel, out_shape=(jax.ShapeDtypeStruct((KS, 2, 8, W), F32...]
where the time goes in v2:
time: 71.9 us; the launch traced here: 71.4 us
  Pallas kernels  67.9 us (94%)
  local copies, waits for them, and re-layouts  2.91 us (4%)
    pallas_call x1, Pallas kernels, per_device(): pl.pallas_call(kernel, out_shape=(jax.ShapeDtypeStruct((KS, 2, 8, W), F32...  67.9 us
    unnamed x2, local copies, waits for them, and re-layouts  2.91 us

profile of v2, /device:TPU:1, one launch (start us, length us, event | category | flops | bytes accessed | tf_op | source)
XLA Modules:
  0.0 71.4 jit_solution(12534113988286038419)
XLA Ops:
  0.6 67.9 %selinv.1 = (f32[4,2,8,256]{3,2,1,0:T(8,128)}, f32[64,32]{1,0:T(8,128)}) custom-call(bf16[2,256,256]{2,1,0:T(8,128)(2,1)} %bitcast.5, bf16[4,2,8,256]{3,2,1,0:T(8,128)(2,1)} %bitcast.7, s32[4,32]{1,0:T(4,128)} %anc_ref.1, bf16[6,256,256]{2,1,0:T(8,128)(2,1)} %l_ref.1, bf16[4,256,256]{2,1,0:T(8,128)(2,1)} %d_ref.1), custom_call_target="tpu_custom_call" | custom-call | tf_op jit(solution)/shard_map/selinv/pallas_call | solution.py:409
  68.5 1.4 %copy.8 = f32[64,32]{0,1:T(8,128)} copy(f32[64,32]{1,0:T(8,128)} %get-tuple-element.7) | data formatting | bytes 16384
  69.9 1.5 %copy.10 = f32[4,2,1,8,256]{4,3,2,1,0:T(8,128)} copy(f32[4,2,1,8,256]{4,3,2,1,0:T(8,128)} %bitcast.6) | data formatting | bytes 131072

commit v3 on v2

--- a/solution.py
+++ b/solution.py
@@ -46,8 +46,9 @@
 
 
 def kernel(
-    s_ref, p_ref, anc_ref, l_ref, d_ref, y_ref, v_ref,
-    fg, wide, st, give, keep, pairb, red, mh, ml, uh, ul, ysend, yrecv, vsend, vrecv, wc, dm, dmw, vps, vpr,
+    s_in, p_in, anc_in, l_in, d_in, y_ref, v_ref,
+    s_ref, p_ref, anc_ref, l_ref, d_ref,
+    fg, wide, st, give, keep, pairb, red, mh, ml, uh, ul, ysend, yrecv, vsend, vrecv, wc, dm, dmw, dpart, vps, vpr, in_sem,
     ag_send, ag_recv, ye_send, ye_recv, pair_send, pair_recv, red_send, red_recv,
     y_send, y_recv, v_send, v_recv, f_send, f_recv,
 ):
@@ -58,6 +59,11 @@
     ylo = div(q, NZ)
     z = rem(q, NZ)
 
+    pairs = ((p_in, p_ref), (anc_in, anc_ref), (s_in, s_ref), (l_in, l_ref), (d_in, d_ref))
+    fetches = [pltpu.make_async_copy(a, b, in_sem.at[n]) for n, (a, b) in enumerate(pairs)]
+    for fetch in fetches:
+        fetch.start()
+
     def copy(src, dst, send, recv, prow, pcol):
         return pltpu.make_async_remote_copy(
             src_ref=src, dst_ref=dst, send_sem=send, recv_sem=recv,
@@ -71,12 +77,14 @@
     for other in greeted:
         pl.semaphore_signal(barrier, inc=1, device_id=other, device_id_type=MESH)
 
+    fetches[0].wait()
+    fetches[1].wait()
     for k in range(KS):
         parts = []
         for r in range(2):
             flag = anc_ref[k, r * NP + p].astype(F32)
             parts.append(p_ref[k, r].astype(F32) * flag)
-        fg[z, ylo, k] = jnp.concatenate(parts, axis=0).astype(BF16)
+        fg[ylo, z, k] = jnp.concatenate(parts, axis=0).astype(BF16)
 
     pl.semaphore_wait(barrier, len(greeted))
 
@@ -118,14 +126,14 @@
     def hop(a, b):
         at = rem(z + NZ - a, NZ)
         return copy(
-            fg.at[at, ylo], fg.at[at, ylo], ag_send.at[a + b + 7], ag_recv.at[a + b + 7],
+            fg.at[ylo, at], fg.at[ylo, at], ag_send.at[a + b + 7], ag_recv.at[a + b + 7],
             p, ylo * NZ + rem(z + NZ + b, NZ),
         )
 
     def across(a):
         at = rem(z + NZ - a, NZ)
         return copy(
-            fg.at[at, ylo], fg.at[at, ylo], ye_send.at[a + 7], ye_recv.at[a + 7], p, (1 - ylo) * NZ + z
+            fg.at[ylo, at], fg.at[ylo, at], ye_send.at[a + 7], ye_recv.at[a + 7], p, (1 - ylo) * NZ + z
         )
 
     relays = {3: (3, 1, -1), -3: (-3, 1, -1), 6: (2, 1, -1), -6: (-1, 1)}
@@ -133,14 +141,17 @@
 
     def task_s(r):
         def run():
+            if r == 0:
+                fetches[2].wait()
             value = s_ref[r].astype(F32).reshape(2, NZ, 8, W)
             for y in range(2):
-                wide[:, y, r] = value[y]
+                wide[y, :, r] = value[y]
 
         return run
 
     def task_t():
-        st[...] = wide[...].reshape(512, W).T.astype(BF16)
+        for y in range(2):
+            st[y] = wide[y].reshape(W, W).T.astype(BF16)
 
     def put(m, k, value):
         high, low = halves(value)
@@ -158,6 +169,7 @@
         return l_ref[pair_index(m, k)].astype(F32)
 
     def task_zero():
+        fetches[3].wait()
         rows_at = lax.broadcasted_iota(jnp.int32, (W, W), 0)
         cols_at = lax.broadcasted_iota(jnp.int32, (W, W), 1)
         eye = jnp.where(rows_at == cols_at, 1.0, 0.0).astype(BF16)
@@ -182,6 +194,7 @@
     lane = lax.broadcasted_iota(jnp.int32, (32, 128), 1)
 
     def task_d():
+        fetches[4].wait()
         dd = d_ref[block, pl.ds(first, 32), :]
         for a in range(8):
             cols = slice(128 * a, 128 * a + 128)
@@ -201,11 +214,13 @@
         picked = jnp.where(lane < 64, picked, 0.0)
         high = picked.astype(BF16).astype(F32)
         dmw[...] = jnp.where(lane < 64, high, pltpu.roll(picked - high, 64, 1)).astype(BF16)
-
-    def task_wc():
-        wc[...] = jnp.zeros(wc.shape, F32)
-
-    tasks = [task_s(0), task_s(1), task_t, task_zero, task_m2, task_m3, task_d, task_wc]
+        for k in range(KS):
+            cols = slice(k * W, (k + 1) * W)
+            dpart[k] = dot_rows(mh[block, pl.ds(first, 32), cols], dmw[...]) + dot_rows(
+                ml[block, pl.ds(first, 32), cols], dmw[...]
+            )
+
+    tasks = [task_s(0), task_s(1), task_t, task_zero, task_m2, task_m3, task_d]
 
     for a in direct:
         hop(0, a).start()
@@ -218,6 +233,15 @@
         across(a).start()
         if tasks and a in (1, -1, -2, -4, -6):
             tasks.pop(0)()
+    mine = pl.multiple_of(core * 128, 128)
+    theirs = pl.multiple_of((1 - core) * 128, 128)
+
+    def half(first_row, row, k):
+        return dot(st[row, pl.ds(first_row, 128), :], fg[row, :, k].reshape(W, W))
+
+    for k in range(KS):
+        give[k] = half(theirs, ylo, k)
+        keep[k] = half(mine, ylo, k)
     while tasks:
         tasks.pop(0)()
     for a in range(-7, 9):
@@ -226,16 +250,17 @@
     def gathered(k):
         return fg[:, :, k].reshape(512, W)
 
-    mine = pl.multiple_of(core * 128, 128)
-    theirs = pl.multiple_of((1 - core) * 128, 128)
     mate = p + 1 - 2 * core
 
     def pair(k):
         return copy(give.at[k], pairb.at[k], pair_send.at[k], pair_recv.at[k], mate, q)
 
+    def slot(at):
+        return rem(at + NZ - z, 8)
+
     def spread(k, d):
         to = rem(chip + d, 8)
-        rows_to = pl.multiple_of(to * 16, 16)
+        rows_to = pl.multiple_of(slot(to) * 16, 16)
         return copy(
             keep.at[k, pl.ds(rows_to, 16)], red.at[k, d - 1], red_send.at[k], red_recv.at[k],
             to * 2 + core, q,
@@ -248,27 +273,24 @@
             spread(k, d).start()
 
     for k in range(KS):
-        give[k] = dot(st[pl.ds(theirs, 128), :], gathered(k))
-        keep[k] = dot(st[pl.ds(mine, 128), :], gathered(k))
+        give[k] = give[k] + half(theirs, 1 - ylo, k)
+        keep[k] = keep[k] + half(mine, 1 - ylo, k)
         pair(k).start()
         if k:
             pass_on(k - 1)
     pass_on(KS - 1)
     for k in range(KS):
-        if k == 0:
-            uh[0] = gathered(0)
-            ul[0] = jnp.zeros((512, W), BF16)
-        else:
-            total = gathered(k).astype(F32)
-            for m in range(k):
-                left_side = gathered(m)
-                cols = slice(k * W, (k + 1) * W)
-                total = total + dot(left_side, mh[m, :, cols]) + dot(left_side, ml[m, :, cols])
-            high, low = halves(total)
-            uh[k] = high
-            ul[k] = low
-
-    own_rows = pl.multiple_of(chip * 16, 16)
+        total = gathered(k).astype(F32)
+        for m in range(k):
+            left_side = gathered(m)
+            cols = slice(k * W, (k + 1) * W)
+            total = total + dot(left_side, mh[m, :, cols]) + dot(left_side, ml[m, :, cols])
+        wide[...] = total.reshape(2, NZ, 2, 8, W)
+        high, low = halves(wide[:, :, ylo].reshape(W, W).T)
+        uh[k] = high
+        ul[k] = low
+
+    own_rows = pl.multiple_of(slot(chip) * 16, 16)
     blocks = []
     for k in range(KS):
         drain(red.at[k], red_recv.at[k])
@@ -300,7 +322,7 @@
             )
             vsend[4 * a + b] = piece
 
-    chunk = core * 8 + chip
+    chunk = core * 8 + slot(chip)
     here = z == p
 
     def ypart(e):
@@ -353,14 +375,11 @@
             high = value.astype(BF16).astype(F32)
             value = jnp.where(wide_lane < 64, high, pltpu.roll(value - high, 64, 2))
             for n in range(8):
-                wc[2 * n + h, y, ylo] = value[n]
-    columns = wc[...].reshape(512, 128).astype(BF16)
+                wc[y, 2 * n + h] = value[n]
+    columns = wc[...].reshape(W, 128).astype(BF16)
     lane16 = lax.broadcasted_iota(jnp.int32, (4, 16, 128), 2)
     for k in range(KS):
-        cols = slice(k * W, (k + 1) * W)
-        total = dot_rows(uh[k], columns) + dot_rows(ul[k], columns)
-        total = total + dot_rows(mh[block, pl.ds(first, 32), cols], dmw[...])
-        total = total + dot_rows(ml[block, pl.ds(first, 32), cols], dmw[...])
+        total = dot(uh[k], columns) + dot(ul[k], columns) + dpart[k]
         total = total + pltpu.roll(total, 64, 1)
         total = total.reshape(4, 4, 16, 128)
         for e in range(2):
@@ -395,13 +414,18 @@
     total = vps[p, ylo]
     for n in range(31):
         total = total + vpr[n]
-    for g in range(4):
-        value = total
-        if g:
-            value = pltpu.roll(value, 128 - 32 * g, 1)
-        v_ref[16 * g : 16 * g + 16, :] = value[:, :32]
+    parts = [total] + [pltpu.roll(total, 128 - 32 * g, 1) for g in range(1, 4)]
+    v_ref[...] = jnp.concatenate(parts, axis=0).T[:32]
 
     finish(6)
+
+
+def hand_out(y_in, v_in, y_out, v_out, sem):
+    copies = [pltpu.make_async_copy(y_in, y_out, sem.at[0]), pltpu.make_async_copy(v_in, v_out, sem.at[1])]
+    for one in copies:
+        one.start()
+    for one in copies:
+        one.wait()
 
 
 def per_device(sep_inverse, panels, ancestors, window_factor, diag_inverse):
@@ -409,38 +433,39 @@
     ys, window = pl.pallas_call(
         kernel,
         out_shape=(
-            jax.ShapeDtypeStruct((KS, 2, 8, W), F32),
-            jax.ShapeDtypeStruct((64, 32), F32),
+            pltpu.VMEM((KS, 2, 8, W), F32),
+            pltpu.VMEM((32, 64), F32),
         ),
-        in_specs=[
-            pl.BlockSpec(memory_space=pltpu.VMEM),
-            pl.BlockSpec(memory_space=pltpu.VMEM),
-            pl.BlockSpec(memory_space=pltpu.SMEM),
-            pl.BlockSpec(memory_space=pltpu.VMEM),
-            pl.BlockSpec(memory_space=pltpu.VMEM),
-        ],
+        in_specs=[pl.BlockSpec(memory_space=pl.ANY)] * 5,
         out_specs=(pl.BlockSpec(memory_space=pltpu.VMEM), pl.BlockSpec(memory_space=pltpu.VMEM)),
         scratch_shapes=[
-            pltpu.VMEM((NZ, 2, KS, 16, W), BF16),
-            pltpu.VMEM((NZ, 2, 2, 8, W), F32),
-            pltpu.VMEM((W, 512), BF16),
+            pltpu.VMEM((2, W, W), BF16),
+            pltpu.VMEM((KS, 2, 8, W), BF16),
+            pltpu.SMEM((KS, 2 * NP), jnp.int32),
+            pltpu.VMEM((6, W, W), BF16),
+            pltpu.VMEM((KS, W, W), BF16),
+            pltpu.VMEM((2, NZ, KS, 16, W), BF16),
+            pltpu.VMEM((2, NZ, 2, 8, W), F32),
+            pltpu.VMEM((2, W, W), BF16),
             pltpu.VMEM((KS, 128, W), F32),
             pltpu.VMEM((KS, 128, W), F32),
             pltpu.VMEM((KS, 128, W), F32),
             pltpu.VMEM((KS, 7, 16, W), F32),
             pltpu.VMEM((KS, W, NC), BF16),
             pltpu.VMEM((KS, W, NC), BF16),
-            pltpu.VMEM((KS, 512, W), BF16),
-            pltpu.VMEM((KS, 512, W), BF16),
+            pltpu.VMEM((KS, W, W), BF16),
+            pltpu.VMEM((KS, W, W), BF16),
             pltpu.VMEM((2, 8, NC), F32),
             pltpu.VMEM((2, 8, NC), F32),
             pltpu.VMEM((NZ, 8, 128), F32),
             pltpu.VMEM((NZ, 8, 128), F32),
-            pltpu.VMEM((NZ, 2, 2, 8, 128), F32),
+            pltpu.VMEM((2, NZ, 8, 128), F32),
             pltpu.VMEM((8, 32, 128), F32),
             pltpu.VMEM((32, 128), BF16),
+            pltpu.VMEM((KS, W, 128), F32),
             pltpu.VMEM((NP, 2, 16, 128), F32),
             pltpu.VMEM((31, 16, 128), F32),
+            dma((5,)),
             dma((16,)), dma((16,)),
             dma((16,)), dma((16,)),
             dma((KS,)), dma((KS,)),
@@ -458,7 +483,22 @@
         window_factor,
         diag_inverse,
     )
-    return ys.reshape(KS, 2, 1, 8, W), window
+    vmem = pl.BlockSpec(memory_space=pltpu.VMEM)
+    ys, window = pl.pallas_call(
+        hand_out,
+        out_shape=(
+            jax.ShapeDtypeStruct((KS, 2, 8, W), F32),
+            jax.ShapeDtypeStruct((32, 64), F32),
+        ),
+        in_specs=[vmem, vmem],
+        out_specs=(pl.BlockSpec(memory_space=pl.ANY),) * 2,
+        scratch_shapes=[pltpu.SemaphoreType.DMA((2,))],
+        name="hand_out",
+    )(
+        pltpu.with_memory_space_constraint(ys, pltpu.VMEM),
+        pltpu.with_memory_space_constraint(window, pltpu.VMEM),
+    )
+    return ys.reshape(KS, 2, 1, 8, W), window.T
 
 
 def solution(mesh):

time: 71.9 us -> 63.9 us (0.89)
  Pallas kernels: 67.9 us -> 63.1 us
  local copies, waits for them, and re-layouts: 2.91 us -> 0 us
    pallas_call x1 -> x2, Pallas kernels: 67.9 us -> 63.1 us  [the longest x1 62.5 us: per_device(): pl.pallas_call(kernel, out_shape=(pltpu.VMEM((KS, 2, 8, W), F32), pltpu.V...]
    unnamed x2 -> x0, local copies, waits for them, and re-layouts: 2.91 us -> none
where the time goes in v3:
time: 63.9 us; the launch traced here: 63.8 us
  Pallas kernels  63.1 us (99%)
  between operations  0.64 us (1%)
    pallas_call x1, Pallas kernels, per_device(): pl.pallas_call(kernel, out_shape=(pltpu.VMEM((KS, 2, 8, W), F32), pltpu.V...  62.5 us

profile of v3, /device:TPU:1, one launch (start us, length us, event | category | flops | bytes accessed | tf_op | source)
XLA Modules:
  0.0 63.8 jit_solution(14927557346329592252)
XLA Ops:
  0.6 62.5 %selinv.1 = (f32[4,2,8,256]{3,2,1,0:T(8,128)S(1)}, f32[32,64]{1,0:T(8,128)S(1)}) custom-call(bf16[2,256,256]{2,1,0:T(8,128)(2,1)} %bitcast.6, bf16[4,2,8,256]{3,2,1,0:T(8,128)(2,1)} %bitcast.7, s32[4,32]{1,0:T(4,128)} %anc_in.1, bf16[6,256,256]{2,1,0:T(8,128)(2,1)} %l_in.1, bf16[4,256,256]{2,1,0:T(8,128)(2,1)} %d_in.1), custom_call_target="tpu_custom_call" | custom-call | tf_op jit(solution)/shard_map/selinv/pallas_call | solution.py:433
  63.1 0.7 %hand_out.1 = (f32[4,2,8,256]{3,2,1,0:T(8,128)}, f32[32,64]{1,0:T(8,128)}) custom-call(f32[4,2,8,256]{3,2,1,0:T(8,128)S(1)} %get-tuple-element.6.y_in, f32[32,64]{1,0:T(8,128)S(1)} %get-tuple-element.7.v_in), custom_call_target="tpu_custom_call" | custom-call | tf_op jit(solution)/shard_map/hand_out/pallas_call | solution.py:487

commit v4 on v3

--- a/solution.py
+++ b/solution.py
@@ -74,6 +74,7 @@
     greeted = [(p + 1 - 2 * core, q), (p, (1 - ylo) * NZ + z)]
     greeted += [(rem(chip + d, 8) * 2 + core, q) for d in range(1, 8)]
     greeted += [(p, ylo * NZ + rem(z + NZ + a, NZ)) for a in (1, -1, 3, -3, -2)]
+    greeted += [(p, (1 - ylo) * NZ + rem(z + NZ + a, NZ)) for a in (1, -1, -2)]
     for other in greeted:
         pl.semaphore_signal(barrier, inc=1, device_id=other, device_id_type=MESH)
 
@@ -130,6 +131,13 @@
             p, ylo * NZ + rem(z + NZ + b, NZ),
         )
 
+    def slant(a, b):
+        at = rem(z + NZ - a, NZ)
+        return copy(
+            fg.at[ylo, at], fg.at[ylo, at], ye_send.at[a + b + 7], ye_recv.at[a + b + 7],
+            p, (1 - ylo) * NZ + rem(z + NZ + b, NZ),
+        )
+
     def across(a):
         at = rem(z + NZ - a, NZ)
         return copy(
@@ -138,6 +146,7 @@
 
     relays = {3: (3, 1, -1), -3: (-3, 1, -1), 6: (2, 1, -1), -6: (-1, 1)}
     direct = (3, -3, 1, -1)
+    tail = (5, -5, 7, -7, 8)
 
     def task_s(r):
         def run():
@@ -220,7 +229,7 @@
                 ml[block, pl.ds(first, 32), cols], dmw[...]
             )
 
-    tasks = [task_s(0), task_s(1), task_t, task_zero, task_m2, task_m3, task_d]
+    tasks = [task_s(0), task_s(1), task_t]
 
     for a in direct:
         hop(0, a).start()
@@ -230,9 +239,15 @@
         hop(0, a).wait_recv()
         for b in relays.get(a, ()):
             hop(a, b).start()
-        across(a).start()
-        if tasks and a in (1, -1, -2, -4, -6):
+        if abs(a) == 6:
+            for b in relays[a]:
+                slant(a, b).start()
+        if a not in tail:
+            across(a).start()
+        if tasks and a in (-3, -6):
             tasks.pop(0)()
+    while tasks:
+        tasks.pop(0)()
     mine = pl.multiple_of(core * 128, 128)
     theirs = pl.multiple_of((1 - core) * 128, 128)
 
@@ -258,8 +273,11 @@
     def slot(at):
         return rem(at + NZ - z, 8)
 
+    offsets = ((1, 2), (1, 1), (1, 3), (1, 0), (0, 2), (0, 1), (0, 3))
+
     def spread(k, d):
-        to = rem(chip + d, 8)
+        dy, dx = offsets[d - 1]
+        to = rem(div(chip, 4) + dy, 2) * 4 + rem(chip + dx, 4)
         rows_to = pl.multiple_of(slot(to) * 16, 16)
         return copy(
             keep.at[k, pl.ds(rows_to, 16)], red.at[k, d - 1], red_send.at[k], red_recv.at[k],
@@ -279,16 +297,9 @@
         if k:
             pass_on(k - 1)
     pass_on(KS - 1)
-    for k in range(KS):
-        total = gathered(k).astype(F32)
-        for m in range(k):
-            left_side = gathered(m)
-            cols = slice(k * W, (k + 1) * W)
-            total = total + dot(left_side, mh[m, :, cols]) + dot(left_side, ml[m, :, cols])
-        wide[...] = total.reshape(2, NZ, 2, 8, W)
-        high, low = halves(wide[:, :, ylo].reshape(W, W).T)
-        uh[k] = high
-        ul[k] = low
+    task_zero()
+    task_m2()
+    task_m3()
 
     own_rows = pl.multiple_of(slot(chip) * 16, 16)
     blocks = []
@@ -341,7 +352,7 @@
     def vlocal():
         return pltpu.make_async_copy(vsend.at[z], vrecv.at[chunk], v_recv)
 
-    for d in range(1, NZ):
+    for d in (8, 7, 9, 6, 10, 5, 11, 4, 12, 3, 13, 2, 14, 1, 15):
         vpart(d).start()
 
     @pl.when(here)
@@ -362,6 +373,18 @@
         @pl.when(jnp.logical_not(home))
         def _():
             ypart(e).start()
+
+    task_d()
+    for k in range(KS):
+        total = gathered(k).astype(F32)
+        for m in range(k):
+            left_side = gathered(m)
+            cols = slice(k * W, (k + 1) * W)
+            total = total + dot(left_side, mh[m, :, cols]) + dot(left_side, ml[m, :, cols])
+        wide[...] = total.reshape(2, NZ, 2, 8, W)
+        high, low = halves(wide[:, :, ylo].reshape(W, W).T)
+        uh[k] = high
+        ul[k] = low
 
     drain(vrecv, v_recv)
     got = vrecv[...].reshape(2, 8, 8, 128)
@@ -392,17 +415,21 @@
                 packed = value if packed is None else jnp.where(lane16 < 32 * g, packed, value)
             vps[4 * k : 4 * k + 4, e] = packed
 
-    def final(dp, dy):
-        to = rem(p + dp, NP)
-        row = rem(ylo + dy, 2)
-        return copy(
-            vps.at[to, row], vpr.at[2 * dp + dy - 1], f_send, f_recv, to, row * NZ + z
-        )
-
-    for dp in range(NP):
-        for dy in range(2):
-            if dp or dy:
-                final(dp, dy).start()
+    plane = [
+        (dyh, dyl, dx, dc) for dyh in range(2) for dyl in range(2) for dx in range(4) for dc in range(2)
+    ]
+    plane = sorted(
+        plane[1:], key=lambda o: (1 if o[1] else 2 * o[0]) + min(o[2], 4 - o[2]), reverse=True
+    )
+
+    def final(n):
+        dyh, dyl, dx, dc = plane[n]
+        to = rem(div(p, 8) + dyh, 2) * 8 + rem(chip + dx, 4) * 2 + rem(core + dc, 2)
+        row = rem(ylo + dyl, 2)
+        return copy(vps.at[to, row], vpr.at[n], f_send, f_recv, to, row * NZ + z)
+
+    for n in range(len(plane)):
+        final(n).start()
 
     for r in range(2):
         drain(yrecv.at[r], y_recv.at[r])

time: 63.9 us -> 60.3 us (0.944)
  Pallas kernels: 63.1 us -> 59.6 us
    pallas_call x1, Pallas kernels: 62.5 us -> 58.9 us  [per_device(): pl.pallas_call(kernel, out_shape=(pltpu.VMEM((KS, 2, 8, W), F32), pltpu.V...]
where the time goes in v4:
time: 60.3 us; the launch traced here: 60.2 us
  Pallas kernels  59.6 us (99%)
  between operations  0.64 us (1%)
    pallas_call x1, Pallas kernels, per_device(): pl.pallas_call(kernel, out_shape=(pltpu.VMEM((KS, 2, 8, W), F32), pltpu.V...  58.9 us

profile of v4, /device:TPU:1, one launch (start us, length us, event | category | flops | bytes accessed | tf_op | source)
XLA Modules:
  0.0 60.2 jit_solution(4839463727851085871)
XLA Ops:
  0.6 58.9 %selinv.1 = (f32[4,2,8,256]{3,2,1,0:T(8,128)S(1)}, f32[32,64]{1,0:T(8,128)S(1)}) custom-call(bf16[2,256,256]{2,1,0:T(8,128)(2,1)} %bitcast.6, bf16[4,2,8,256]{3,2,1,0:T(8,128)(2,1)} %bitcast.7, s32[4,32]{1,0:T(4,128)} %anc_in.1, bf16[6,256,256]{2,1,0:T(8,128)(2,1)} %l_in.1, bf16[4,256,256]{2,1,0:T(8,128)(2,1)} %d_in.1), custom_call_target="tpu_custom_call" | custom-call | tf_op jit(solution)/shard_map/selinv/pallas_call | solution.py:460
  59.6 0.7 %hand_out.1 = (f32[4,2,8,256]{3,2,1,0:T(8,128)}, f32[32,64]{1,0:T(8,128)}) custom-call(f32[4,2,8,256]{3,2,1,0:T(8,128)S(1)} %get-tuple-element.6.y_in, f32[32,64]{1,0:T(8,128)S(1)} %get-tuple-element.7.v_in), custom_call_target="tpu_custom_call" | custom-call | tf_op jit(solution)/shard_map/hand_out/pallas_call | solution.py:514

commit v5 on v4

--- a/solution.py
+++ b/solution.py
@@ -235,7 +235,7 @@
         hop(0, a).start()
     across(0).start()
     tasks.pop(0)()
-    for a in (1, -1, 3, -3, 2, -2, 4, -4, 6, -6, 5, -5, 7, -7, 8):
+    for a in (1, -1, 3, -3, 6, -6, 2, -2, 4, -4, 5, -5, 7, -7, 8):
         hop(0, a).wait_recv()
         for b in relays.get(a, ()):
             hop(a, b).start()

time: 60.3 us -> 60.3 us (level)
  no operation moved by 1% of the time
where the time goes in v5:
time: 60.3 us; the launch traced here: 60.2 us
  Pallas kernels  59.5 us (99%)
  between operations  0.64 us (1%)
    pallas_call x1, Pallas kernels, per_device(): pl.pallas_call(kernel, out_shape=(pltpu.VMEM((KS, 2, 8, W), F32), pltpu.V...  58.9 us

profile of v5, /device:TPU:1, one launch (start us, length us, event | category | flops | bytes accessed | tf_op | source)
XLA Modules:
  0.0 60.2 jit_solution(15061504321644162679)
XLA Ops:
  0.6 58.9 %selinv.1 = (f32[4,2,8,256]{3,2,1,0:T(8,128)S(1)}, f32[32,64]{1,0:T(8,128)S(1)}) custom-call(bf16[2,256,256]{2,1,0:T(8,128)(2,1)} %bitcast.6, bf16[4,2,8,256]{3,2,1,0:T(8,128)(2,1)} %bitcast.7, s32[4,32]{1,0:T(4,128)} %anc_in.1, bf16[6,256,256]{2,1,0:T(8,128)(2,1)} %l_in.1, bf16[4,256,256]{2,1,0:T(8,128)(2,1)} %d_in.1), custom_call_target="tpu_custom_call" | custom-call | tf_op jit(solution)/shard_map/selinv/pallas_call | solution.py:460
  59.5 0.7 %hand_out.1 = (f32[4,2,8,256]{3,2,1,0:T(8,128)}, f32[32,64]{1,0:T(8,128)}) custom-call(f32[4,2,8,256]{3,2,1,0:T(8,128)S(1)} %get-tuple-element.6.y_in, f32[32,64]{1,0:T(8,128)S(1)} %get-tuple-element.7.v_in), custom_call_target="tpu_custom_call" | custom-call | tf_op jit(solution)/shard_map/hand_out/pallas_call | solution.py:514
